TPU v7x, 32 devices: a whole 2x2x4 slice. The times are simulated.
32 devices in a mesh: row: 4 (over z), col: 8 (over y, x, core).
Axes of the slice: x: 2, y: 2, z: 4, core: 2. Of those that a mesh axis runs over, the one named last changes fastest.
Arguments:
- hessian: float32 [18432, 18432], P('row', 'col'), may hold values from -1 to 5, as said below
- right_side: float32 [18432, 512], P('row'), may hold values from -6 to 6
- mask: int32 [18432, 512], P('row'), may hold values 0 or 1
- damping: float32 [1], replicated, may hold values from 0.4 to 1.2
Outputs:
- solution: float32 [18432, 512], P('row')
Inputs may be any that keep to these rules, and one draw needn't show every extreme that they name: hessian is symmetric and positive definite.
All inputs are finite; a program needn't handle non-finite values. No bound on the sum of `mask` on one device may be relied on, other than what follows from the above.
Results may differ from a plain program's by a relative error of at most 0.0001.
Values sent between devices are 32-bit elements; how exact they have to be, the bound alone decides.
No kernel may reach another device: no remote copies, remote signals or barrier semaphores. Data moves between devices by JAX's collectives and lax.ppermute only.
A program may use at most 192 MiB of HBM per device.

v0:
```python
import jax
import jax.numpy as jnp
from jax import lax
from jax.sharding import PartitionSpec as P

ITERS = 3
epsilon = 1e-06


def from_root(block, axis, source):
    block = jnp.where(lax.axis_index(axis) == source, block, jnp.zeros_like(block))
    return lax.psum(block, axis)


def column_sums(first, second):
    return jnp.sum(first * second, axis=0)


def both_sums(residual, applied):
    return lax.psum((column_sums(residual, residual), column_sums(residual, applied)), "row")


def on_device(hessian, right_side, mask, damping):
    mask_float = mask.astype(jnp.float32)
    damping_value = damping[0]
    blocks_ratio = lax.axis_size("col") // lax.axis_size("row")
    block_width = hessian.shape[1]
    col_position = lax.axis_index("col")

    def masked_apply(vector):
        own_slice = lax.dynamic_slice_in_dim(
            vector, col_position % blocks_ratio * block_width, block_width, 0
        )
        column_block = from_root(own_slice, "row", col_position // blocks_ratio)
        partial_value = jnp.dot(
            hessian,
            column_block,
            precision=lax.Precision.HIGHEST,
            preferred_element_type=jnp.float32,
        )
        summed = lax.psum(partial_value, "col")
        return mask_float * (summed + damping_value * vector)

    residual = mask_float * right_side
    direction = residual
    solution = jnp.zeros_like(right_side)
    applied = masked_apply(residual)
    norm_now, inner = both_sums(residual, applied)
    step_size = norm_now / (inner + epsilon)
    along = applied
    for iteration in range(ITERS):
        solution = solution + step_size * direction
        residual = residual - step_size * along
        if iteration + 1 < ITERS:
            applied = masked_apply(residual)
            norm_next, inner = both_sums(residual, applied)
            factor = norm_next / (norm_now + epsilon)
            curvature = inner - factor * norm_next / step_size
            step_size = norm_next / (curvature + epsilon)
            direction = residual + factor * direction
            along = applied + factor * along
            norm_now = norm_next
    return solution


def solution(mesh):
    in_specs = (P("row", "col"), P("row", None), P("row", None), P())
    out_specs = P("row", None)
    return jax.shard_map(
        on_device, mesh=mesh, in_specs=in_specs, out_specs=out_specs, check_vma=False
    )
```

profile of v0, /device:TPU:0, one launch (start us, length us, event | category | flops | bytes accessed | tf_op | source)
XLA Modules:
  0.0 1330.0 jit_solution(18420275999820878551)
XLA Ops:
  6.5 0.0 all-reduce.10.cloned.1.call-start
  6.5 9.6 copy.5
  16.2 9.6 copy.6
  25.7 11.9 convert_multiply_fusion
  37.7 4.9 dynamic-slice_select_fusion.2
  42.6 0.0 all-reduce.10.cloned.1.call-update
  42.6 0.0 all-reduce.12.cloned.1.call-start
  42.6 174.8 %all-reduce.10.cloned.1.call-done = f32[2304,512]{0,1:T(8,128)} async-done(((f32[2304,512]{0,1:T(8,128)}), f32[2304,512]{0,1:T(8,128)}) %all-reduce.10.cloned.1.call-update) | async-done | bytes 4718608 | tf_op jit(solution)/shard_map/psum | solution.py:12
  217.4 75.6 %convolution_bitcast_fusion.2 = f32[4608,512]{0,1:T(8,128)} fusion(f32[2304,512]{0,1:T(8,128)} %all-reduce.10.cloned.1.call-done, f32[4608,2304]{1,0:T(8,128)} %param.4), kind=kOutput, calls=%fused_computation.14 | convolution fusion | flops 65229815808 | bytes 56623104 | tf_op jit(solution)/shard_map/dot_general | solution.py:35
  293.0 0.0 all-reduce.12.cloned.1.call-update
  293.0 0.0 all-reduce.14.cloned.1.call-start
  293.7 136.0 %all-reduce.12.cloned.1.call-done = f32[4608,512]{0,1:T(8,128)} async-done(((f32[4608,512]{0,1:T(8,128)}), f32[4608,512]{0,1:T(8,128)}) %all-reduce.12.cloned.1.call-update) | async-done | bytes 9437200 | tf_op jit(solution)/shard_map/psum | solution.py:41
  429.7 10.3 multiply_reduce_fusion.4
  440.1 11.7 all-reduce.2
  451.8 11.1 multiply_subtract_fusion.1
  462.9 0.0 copy-start
  462.9 3.6 copy-done
  466.6 2.5 dynamic-slice_select_fusion.1
  469.1 0.0 all-reduce.14.cloned.1.call-update
  469.1 0.2 all-reduce.16.cloned.1.call-start
  469.3 169.2 %all-reduce.14.cloned.1.call-done = f32[2304,512]{0,1:T(8,128)} async-done(((f32[2304,512]{0,1:T(8,128)}), f32[2304,512]{0,1:T(8,128)}) %all-reduce.14.cloned.1.call-update) | async-done | bytes 4718608 | tf_op jit(solution)/shard_map/psum | solution.py:12
  638.5 75.6 %convolution_bitcast_fusion.1 = f32[4608,512]{0,1:T(8,128)} fusion(f32[2304,512]{0,1:T(8,128)} %all-reduce.14.cloned.1.call-done, f32[4608,2304]{1,0:T(8,128)} %param.4), kind=kOutput, calls=%fused_computation.13 | convolution fusion | flops 65229815808 | bytes 56623104 | tf_op jit(solution)/shard_map/dot_general | solution.py:35
  714.1 0.0 all-reduce.16.cloned.1.call-update
  714.1 0.0 all-reduce.18.cloned.1.call-start
  714.2 136.7 %all-reduce.16.cloned.1.call-done = f32[4608,512]{0,1:T(8,128)} async-done(((f32[4608,512]{0,1:T(8,128)}), f32[4608,512]{0,1:T(8,128)}) %all-reduce.16.cloned.1.call-update) | async-done | bytes 9437200 | tf_op jit(solution)/shard_map/psum | solution.py:41
  850.9 10.2 multiply_reduce_fusion.2
  861.1 11.7 all-reduce.1
  872.8 15.9 %multiply_subtract_fusion = f32[4608,512]{0,1:T(8,128)S(1)} fusion(f32[4608,512]{0,1:T(8,128)} %copy-done, f32[4608,512]{0,1:T(8,128)} %all-reduce.16.cloned.1.call-done, s32[4608,512]{0,1:T(8,128)} %copy.5, f32[512]{0:T(512)S(1)} %get-tuple-element.21, f32[512]{0:T(512)S(1)} %get-tuple-element.17, f32[]{:T(128)} %bitcast.14, ...), kind=kLoop, calls=%fused_computation.3 | loop fusion | flops 25952256 | bytes 56627204 | tf_op jit(solution)/shard_map/sub | solution.py:53
  888.7 0.0 copy-start.1
  888.7 3.7 copy-done.1
  892.5 2.5 dynamic-slice_select_fusion
  895.0 0.0 all-reduce.18.cloned.1.call-update
  895.0 0.3 all-reduce.20.cloned.1.call-start
  895.3 169.1 %all-reduce.18.cloned.1.call-done = f32[2304,512]{0,1:T(8,128)} async-done(((f32[2304,512]{0,1:T(8,128)}), f32[2304,512]{0,1:T(8,128)}) %all-reduce.18.cloned.1.call-update) | async-done | bytes 4718608 | tf_op jit(solution)/shard_map/psum | solution.py:12
  1064.4 75.6 %convolution_bitcast_fusion = f32[4608,512]{0,1:T(8,128)} fusion(f32[2304,512]{0,1:T(8,128)} %all-reduce.18.cloned.1.call-done, f32[4608,2304]{1,0:T(8,128)} %param.4), kind=kOutput, calls=%fused_computation.12 | convolution fusion | flops 65229815808 | bytes 56623104 | tf_op jit(solution)/shard_map/dot_general | solution.py:35
  1140.0 0.0 all-reduce.20.cloned.1.call-update
  1140.0 136.7 %all-reduce.20.cloned.1.call-done = f32[4608,512]{0,1:T(8,128)} async-done(((f32[4608,512]{0,1:T(8,128)}), f32[4608,512]{0,1:T(8,128)}) %all-reduce.20.cloned.1.call-update) | async-done | bytes 9437200 | tf_op jit(solution)/shard_map/psum | solution.py:41
  1276.8 10.2 multiply_reduce_fusion
  1287.0 11.7 all-reduce
  1298.7 14.8 %multiply_add_fusion = f32[4608,512]{0,1:T(8,128)} fusion(f32[4608,512]{0,1:T(8,128)} %copy-done.1, f32[4608,512]{0,1:T(8,128)} %copy-done, f32[4608,512]{0,1:T(8,128)} %convert_multiply_fusion, f32[512]{0:T(512)S(1)} %get-tuple-element.20, f32[512]{0:T(512)S(1)} %get-tuple-element.19, f32[512]{0:T(512)S(1)} %get-tuple-element.21, ...), kind=kLoop, calls=%fused_computation | loop fusion | flops 21233664 | bytes 37758976 | tf_op jit(solution)/shard_map/add | solution.py:52
  1313.6 9.6 copy.7
  (3 shorter events, 0.0 us)
Async XLA Ops:
  6.5 210.9 %all-reduce.10.cloned.1.call-start = ((), (), s32[]{:S(2)}) async-start(), calls=%async_computation | async-start | bytes 9437184 | tf_op jit(solution)/shard_map/psum | solution.py:12
  42.6 387.1 %all-reduce.12.cloned.1.call-start = ((), (), s32[]{:S(2)}) async-start(), calls=%async_computation.1 | async-start | bytes 18874368 | tf_op jit(solution)/shard_map/psum | solution.py:41
  293.0 345.5 %all-reduce.14.cloned.1.call-start = ((), (), s32[]{:S(2)}) async-start(), calls=%async_computation.2 | async-start | bytes 9437184 | tf_op jit(solution)/shard_map/psum | solution.py:12
  462.9 3.7 copy-start
  469.1 381.8 %all-reduce.16.cloned.1.call-start = ((), (), s32[]{:S(2)}) async-start(), calls=%async_computation.3 | async-start | bytes 18874368 | tf_op jit(solution)/shard_map/psum | solution.py:41
  714.1 350.3 %all-reduce.18.cloned.1.call-start = ((), (), s32[]{:S(2)}) async-start(), calls=%async_computation.4 | async-start | bytes 9437184 | tf_op jit(solution)/shard_map/psum | solution.py:12
  888.7 3.7 copy-start.1
  895.0 381.8 %all-reduce.20.cloned.1.call-start = ((), (), s32[]{:S(2)}) async-start(), calls=%async_computation.5 | async-start | bytes 18874368 | tf_op jit(solution)/shard_map/psum | solution.py:41
Sparse Core Ops, SparseCore 0:
  42.7 174.6 all-reduce.9
  293.1 136.5 all-reduce.11
  469.2 169.2 all-reduce.13
  714.3 136.5 all-reduce.15
  895.1 169.2 all-reduce.17
  1140.2 136.5 all-reduce.19
where the time goes:
time: 1330 us
  waiting for transfers between devices  923 us (69%)
  matrix products  227 us (17%)
  other arithmetic  94.6 us (7%)
  local copies, waits for them, and re-layouts  36.2 us (3%)
  blocking collectives  35.1 us (3%)
  between operations  14.2 us (1%)
    psum x3, waiting for transfers between devices, from_root(): return lax.psum(block, axis)  513 us
    psum x3, waiting for transfers between devices, masked_apply(): summed = lax.psum(partial_value, 'col')  409 us
    dot_general x3, matrix products, masked_apply(): jnp.dot(hessian, column_block, precision=lax.Precision.HIGHEST, preferred...  227 us
    psum x3, blocking collectives, both_sums(): lax.psum((column_sums(residual, residual), column_sums(residual, applied)...  35.1 us
    reduce_sum x3, other arithmetic, column_sums(): return jnp.sum(first * second, axis=0)  30.8 us
    sub x2, other arithmetic, on_device(): residual = residual - step_size * along  27 us
  transfers between devices with their start and end apart: 6, of which 6 were waited for; matrix products, arithmetic and copies ran while one was open for 0% of the time, Pallas kernels for 0%

commit v1 on v0

--- a/solution.py
+++ b/solution.py
@@ -5,6 +5,14 @@
 
 ITERS = 3
 epsilon = 1e-06
+
+
+def doubling_sum(x, axis):
+    size, acc = (lax.axis_size(axis), x)
+    for hop in [1 << k for k in range(size.bit_length() - 1)]:
+        pairs = [(i, i ^ hop) for i in range(size)]
+        acc = acc + lax.ppermute(acc, axis, pairs)
+    return acc
 
 
 def from_root(block, axis, source):
@@ -38,7 +46,7 @@
             precision=lax.Precision.HIGHEST,
             preferred_element_type=jnp.float32,
         )
-        summed = lax.psum(partial_value, "col")
+        summed = doubling_sum(partial_value, "col")
         return mask_float * (summed + damping_value * vector)
 
     residual = mask_float * right_side

time: 1330 us -> 2280 us (1.71)
  waiting for transfers between devices: 923 us -> 1780 us
  other arithmetic: 94.6 us -> 176 us
    ppermute x0 -> x9, waiting for transfers between devices: none -> 1260 us  [doubling_sum(): acc = acc + lax.ppermute(acc, axis, pairs)]
    psum x3 -> x0, waiting for transfers between devices: 409 us -> none  [masked_apply(): summed = lax.psum(partial_value, 'col')]
    add x0 -> x6, other arithmetic: none -> 70.3 us  [doubling_sum(): acc = acc + lax.ppermute(acc, axis, pairs)]
  transfers between devices with their start and end apart: 6 -> 12, of which waited for: 6 -> 12; matrix products, arithmetic and copies ran while one was open for 0% -> 0% of each run, Pallas kernels for 0% -> 0%
where the time goes in v1:
time: 2280 us
  waiting for transfers between devices  1780 us (78%)
  matrix products  226 us (10%)
  other arithmetic  176 us (8%)
  local copies, waits for them, and re-layouts  43.4 us (2%)
  blocking collectives  28.4 us (1%)
    ppermute x9, waiting for transfers between devices, doubling_sum(): acc = acc + lax.ppermute(acc, axis, pairs)  1260 us
    psum x3, waiting for transfers between devices, from_root(): return lax.psum(block, axis)  515 us
    dot_general x3, matrix products, masked_apply(): jnp.dot(hessian, column_block, precision=lax.Precision.HIGHEST, preferred...  226 us
    add x6, other arithmetic, doubling_sum(): acc = acc + lax.ppermute(acc, axis, pairs)  70.3 us
  transfers between devices with their start and end apart: 12, of which 12 were waited for; matrix products, arithmetic and copies ran while one was open for 0% of the time, Pallas kernels for 0%

profile of v1, /device:TPU:0, one launch (start us, length us, event | category | flops | bytes accessed | tf_op | source)
XLA Modules:
  0.0 2276.5 jit_solution(11100113205738269379)
XLA Ops:
  6.5 0.0 all-reduce.7.cloned.1.call-start
  6.5 9.6 copy.5
  16.2 9.6 copy.6
  25.7 11.9 convert_multiply_fusion
  37.7 4.8 dynamic-slice_select_fusion.2
  42.5 0.0 all-reduce.7.cloned.1.call-update
  42.5 0.5 all-reduce.9.cloned.1.call-start
  43.0 174.3 %all-reduce.7.cloned.1.call-done = f32[2304,512]{0,1:T(8,128)} async-done(((f32[2304,512]{0,1:T(8,128)}), f32[2304,512]{0,1:T(8,128)}) %all-reduce.7.cloned.1.call-update) | async-done | bytes 4718608 | tf_op jit(solution)/shard_map/psum | solution.py:20
  217.3 75.4 %convolution_bitcast_fusion.2 = f32[4608,512]{0,1:T(8,128)S(1)} fusion(f32[2304,512]{0,1:T(8,128)} %all-reduce.7.cloned.1.call-done, f32[4608,2304]{1,0:T(8,128)} %param.4), kind=kOutput, calls=%fused_computation.14 | convolution fusion | flops 65229815808 | bytes 56623104 | tf_op jit(solution)/shard_map/dot_general | solution.py:43
  292.7 0.0 copy-start.1
  292.8 3.6 copy-done.1
  296.4 0.0 collective-permute-start
  296.4 14.8 collective-permute-done
  311.2 11.8 add.98
  323.0 1.5 collective-permute-start.1
  324.5 203.8 %collective-permute-done.1 = f32[4608,512]{0,1:T(8,128)} collective-permute-done((f32[4608,512]{0,1:T(8,128)}, f32[4608,512]{0,1:T(8,128)}, u32[]{:S(2)}, u32[]{:S(2)}) %collective-permute-start.1) | collective-permute-done | bytes 9437216 | tf_op jit(solution)/shard_map/ppermute | solution.py:14
  528.3 11.8 add.99
  540.1 1.5 collective-permute-start.2
  542.2 202.2 %collective-permute-done.2 = f32[4608,512]{0,1:T(8,128)S(1)} collective-permute-done((f32[4608,512]{0,1:T(8,128)}, f32[4608,512]{0,1:T(8,128)S(1)}, u32[]{:S(2)}, u32[]{:S(2)}) %collective-permute-start.2) | collective-permute-done | bytes 9437216 | tf_op jit(solution)/shard_map/ppermute | solution.py:14
  744.4 14.1 multiply_reduce_fusion.4
  758.5 9.4 all-reduce.2
  767.9 12.5 multiply_subtract_fusion.1
  780.4 4.8 dynamic-slice_select_fusion.1
  785.3 0.0 all-reduce.9.cloned.1.call-update
  785.3 0.2 all-reduce.11.cloned.1.call-start
  785.5 170.5 %all-reduce.9.cloned.1.call-done = f32[2304,512]{0,1:T(8,128)} async-done(((f32[2304,512]{0,1:T(8,128)}), f32[2304,512]{0,1:T(8,128)}) %all-reduce.9.cloned.1.call-update) | async-done | bytes 4718608 | tf_op jit(solution)/shard_map/psum | solution.py:20
  956.0 75.4 %convolution_bitcast_fusion.1 = f32[4608,512]{0,1:T(8,128)S(1)} fusion(f32[2304,512]{0,1:T(8,128)} %all-reduce.9.cloned.1.call-done, f32[4608,2304]{1,0:T(8,128)} %param.4), kind=kOutput, calls=%fused_computation.13 | convolution fusion | flops 65229815808 | bytes 56623104 | tf_op jit(solution)/shard_map/dot_general | solution.py:43
  1031.4 0.0 copy-start.2
  1031.4 3.6 copy-done.2
  1035.0 0.0 collective-permute-start.3
  1035.0 14.8 collective-permute-done.3
  1049.8 11.7 add.103
  1061.5 1.5 collective-permute-start.4
  1062.9 203.8 %collective-permute-done.4 = f32[4608,512]{0,1:T(8,128)} collective-permute-done((f32[4608,512]{0,1:T(8,128)}, f32[4608,512]{0,1:T(8,128)}, u32[]{:S(2)}, u32[]{:S(2)}) %collective-permute-start.4) | collective-permute-done | bytes 9437216 | tf_op jit(solution)/shard_map/ppermute | solution.py:14
  1266.8 11.7 add.104
  1278.4 1.5 collective-permute-start.5
  1279.9 202.8 %collective-permute-done.5 = f32[4608,512]{0,1:T(8,128)S(1)} collective-permute-done((f32[4608,512]{0,1:T(8,128)}, f32[4608,512]{0,1:T(8,128)S(1)}, u32[]{:S(2)}, u32[]{:S(2)}) %collective-permute-start.5) | collective-permute-done | bytes 9437216 | tf_op jit(solution)/shard_map/ppermute | solution.py:14
  1482.8 0.0 copy-start.4
  1482.8 13.8 multiply_reduce_fusion.2
  1496.5 0.0 copy-done.4
  1496.5 9.6 all-reduce.1
  1506.2 15.7 multiply_subtract_fusion
  1521.9 0.0 copy-start
  1521.9 3.7 copy-done
  1525.6 2.5 dynamic-slice_select_fusion
  1528.1 0.0 all-reduce.11.cloned.1.call-update
  1528.2 170.7 %all-reduce.11.cloned.1.call-done = f32[2304,512]{0,1:T(8,128)} async-done(((f32[2304,512]{0,1:T(8,128)}), f32[2304,512]{0,1:T(8,128)}) %all-reduce.11.cloned.1.call-update) | async-done | bytes 4718608 | tf_op jit(solution)/shard_map/psum | solution.py:20
  1698.8 75.4 %convolution_bitcast_fusion = f32[4608,512]{0,1:T(8,128)S(1)} fusion(f32[2304,512]{0,1:T(8,128)} %all-reduce.11.cloned.1.call-done, f32[4608,2304]{1,0:T(8,128)} %param.4), kind=kOutput, calls=%fused_computation.12 | convolution fusion | flops 65229815808 | bytes 56623104 | tf_op jit(solution)/shard_map/dot_general | solution.py:43
  1774.2 0.0 copy-start.3
  1774.3 3.6 copy-done.3
  1777.9 0.0 collective-permute-start.6
  1777.9 14.8 collective-permute-done.6
  1792.6 11.7 add.112
  1804.3 1.5 collective-permute-start.7
  1805.8 203.8 %collective-permute-done.7 = f32[4608,512]{0,1:T(8,128)} collective-permute-done((f32[4608,512]{0,1:T(8,128)}, f32[4608,512]{0,1:T(8,128)}, u32[]{:S(2)}, u32[]{:S(2)}) %collective-permute-start.7) | collective-permute-done | bytes 9437216 | tf_op jit(solution)/shard_map/ppermute | solution.py:14
  2009.6 11.7 add.113
  2021.3 1.5 collective-permute-start.8
  2022.8 202.8 %collective-permute-done.8 = f32[4608,512]{0,1:T(8,128)S(1)} collective-permute-done((f32[4608,512]{0,1:T(8,128)}, f32[4608,512]{0,1:T(8,128)S(1)}, u32[]{:S(2)}, u32[]{:S(2)}) %collective-permute-start.8) | collective-permute-done | bytes 9437216 | tf_op jit(solution)/shard_map/ppermute | solution.py:14
  2225.6 10.3 multiply_reduce_fusion
  2236.0 9.4 all-reduce
  2245.4 14.8 multiply_add_fusion
  2260.2 9.6 copy.7
  (3 shorter events, 0.0 us)
Async XLA Ops:
  6.5 210.8 %all-reduce.7.cloned.1.call-start = ((), (), s32[]{:S(2)}) async-start(), calls=%async_computation | async-start | bytes 9437184 | tf_op jit(solution)/shard_map/psum | solution.py:20
  42.5 913.5 %all-reduce.9.cloned.1.call-start = ((), (), s32[]{:S(2)}) async-start(), calls=%async_computation.1 | async-start | bytes 9437184 | tf_op jit(solution)/shard_map/psum | solution.py:20
  292.7 3.7 copy-start.1
  296.4 14.8 collective-permute-start
  323.0 205.3 %collective-permute-start.1 = (f32[4608,512]{0,1:T(8,128)}, f32[4608,512]{0,1:T(8,128)}, u32[]{:S(2)}, u32[]{:S(2)}) collective-permute-start(f32[4608,512]{0,1:T(8,128)} %add.98), channel_id=1, source_target_pairs={{0,2},{1,3},{2,0},{3,1},{4,6},{5,7},{6,4},{7,5},{8,10},{9,11},{10,... | collective-permute-start | bytes 28311560 | tf_op jit(solution)/shard_map/ppermute | solution.py:14
  540.1 204.3 %collective-permute-start.2 = (f32[4608,512]{0,1:T(8,128)}, f32[4608,512]{0,1:T(8,128)S(1)}, u32[]{:S(2)}, u32[]{:S(2)}) collective-permute-start(f32[4608,512]{0,1:T(8,128)} %add.99), channel_id=1, source_target_pairs={{0,4},{1,5},{2,6},{3,7},{4,0},{5,1},{6,2},{7,3},{8,12},{9,13},{10,... | collective-permute-start | bytes 28311560 | tf_op jit(solution)/shard_map/ppermute | solution.py:14
  785.3 913.5 %all-reduce.11.cloned.1.call-start = ((), (), s32[]{:S(2)}) async-start(), calls=%async_computation.2 | async-start | bytes 9437184 | tf_op jit(solution)/shard_map/psum | solution.py:20
  1031.4 3.6 copy-start.2
  1035.0 14.8 collective-permute-start.3
  1061.5 205.3 %collective-permute-start.4 = (f32[4608,512]{0,1:T(8,128)}, f32[4608,512]{0,1:T(8,128)}, u32[]{:S(2)}, u32[]{:S(2)}) collective-permute-start(f32[4608,512]{0,1:T(8,128)} %add.103), channel_id=1, source_target_pairs={{0,2},{1,3},{2,0},{3,1},{4,6},{5,7},{6,4},{7,5},{8,10},{9,11},{10,... | collective-permute-start | bytes 28311560 | tf_op jit(solution)/shard_map/ppermute | solution.py:14
  1278.4 204.3 %collective-permute-start.5 = (f32[4608,512]{0,1:T(8,128)}, f32[4608,512]{0,1:T(8,128)S(1)}, u32[]{:S(2)}, u32[]{:S(2)}) collective-permute-start(f32[4608,512]{0,1:T(8,128)} %add.104), channel_id=1, source_target_pairs={{0,4},{1,5},{2,6},{3,7},{4,0},{5,1},{6,2},{7,3},{8,12},{9,13},{10,... | collective-permute-start | bytes 28311560 | tf_op jit(solution)/shard_map/ppermute | solution.py:14
  1482.8 13.8 copy-start.4
  1521.9 3.7 copy-start
  1774.2 3.6 copy-start.3
  1777.9 14.8 collective-permute-start.6
  1804.3 205.3 %collective-permute-start.7 = (f32[4608,512]{0,1:T(8,128)}, f32[4608,512]{0,1:T(8,128)}, u32[]{:S(2)}, u32[]{:S(2)}) collective-permute-start(f32[4608,512]{0,1:T(8,128)} %add.112), channel_id=1, source_target_pairs={{0,2},{1,3},{2,0},{3,1},{4,6},{5,7},{6,4},{7,5},{8,10},{9,11},{10,... | collective-permute-start | bytes 28311560 | tf_op jit(solution)/shard_map/ppermute | solution.py:14
  2021.3 204.3 %collective-permute-start.8 = (f32[4608,512]{0,1:T(8,128)}, f32[4608,512]{0,1:T(8,128)S(1)}, u32[]{:S(2)}, u32[]{:S(2)}) collective-permute-start(f32[4608,512]{0,1:T(8,128)} %add.113), channel_id=1, source_target_pairs={{0,4},{1,5},{2,6},{3,7},{4,0},{5,1},{6,2},{7,3},{8,12},{9,13},{10,... | collective-permute-start | bytes 28311560 | tf_op jit(solution)/shard_map/ppermute | solution.py:14
Sparse Core Ops, SparseCore 0:
  42.6 174.6 all-reduce.6
  785.4 170.5 all-reduce.8
  1528.3 170.5 all-reduce.10
